TPU v7x, 512 devices: a whole 4x4x16 slice. The times are simulated.
512 devices in a mesh: dp: 8 (over x, core), tensor: 64 (over z, y).
Axes of the slice: x: 4, y: 4, z: 16, core: 2. Of those that a mesh axis runs over, the one named last changes fastest.
Arguments:
- hidden: bfloat16 [24576, 1536], P(('dp', 'tensor')), parts along dimension 0, may hold values from -13 to 13
- norm_gain: bfloat16 [1536], replicated, may hold values from 0.25 to 1.75
- head_weight: bfloat16 [1536, 49152], P(None, 'tensor'), may hold values from -0.45927933 to 0.45927933
- token_order: int32 [24576], P(('dp', 'tensor')), parts along dimension 0, may hold values from 0 to 3071, each once
- targets: int32 [24576], P(('dp', 'tensor')), parts along dimension 0, may hold values from 0 to 49151
- lengths: int32 [64], P('dp'), parts along dimension 0, may hold values from 1 to 768, 3072 in all
Outputs:
- logprob: float32 [24576], P(('dp', 'tensor')), parts along dimension 0
- entropy: float32 [24576], P(('dp', 'tensor')), parts along dimension 0
- seq_logprob: float32 [64], P('dp'), parts along dimension 0
- seq_entropy: float32 [64], P('dp'), parts along dimension 0
There are 8 independent parts, one for each index of `dp`. A program takes and returns all parts, laid end to end along the dimension named above; an argument that names none is the same for every part. Nothing has to cross between parts.
Inputs may be any that keep to these rules, and one draw needn't show every extreme that they name: Each batch's lengths sum to 3072 and the largest is exactly 768.
All inputs are finite; a program needn't handle non-finite values.
Results may differ from a plain program's by a relative error of at most 0.0011.
Values may be sent and summed in bfloat16 or wider, within the bound.
A program may use at most 64 MiB of HBM per device.

v0:
```python
import jax
import jax.numpy as jnp
from jax import lax
from jax.sharding import PartitionSpec as P


def normalize(rows, norm_gain):
    values = rows.astype(jnp.float32)
    scale = lax.rsqrt(jnp.mean(values * values, axis=-1, keepdims=True) + 1e-05)
    return (values * scale * norm_gain.astype(jnp.float32)).astype(jnp.bfloat16)


def per_device(hidden, norm_gain, head_weight, token_order, targets, lengths):
    slice_width = head_weight.shape[1]
    own_rows = hidden.shape[0]
    vocab_first = lax.axis_index("tensor") * slice_width
    order_all, targets_all = (
        lax.all_gather(token_order, "tensor", axis=0, tiled=True),
        lax.all_gather(targets, "tensor", axis=0, tiled=True),
    )
    wanted_all = targets_all[order_all] - vocab_first
    columns = jnp.arange(slice_width, dtype=jnp.int32)
    normed = normalize(hidden, norm_gain)
    logits = jnp.dot(
        lax.all_gather(normed, "tensor", axis=0, tiled=True),
        head_weight,
        preferred_element_type=jnp.float32,
    )
    local_peak = jnp.max(logits, axis=-1)
    row_peak = lax.pmax(local_peak, "tensor")
    exponent = jnp.exp(logits - row_peak[:, None])
    local_total = jnp.sum(exponent, axis=-1)
    local_weighted = jnp.sum(exponent * logits, axis=-1)
    local_target = jnp.sum(jnp.where(columns[None, :] == wanted_all[:, None], logits, 0.0), axis=-1)
    row_total, row_weighted, target_logit = lax.psum(
        (local_total, local_weighted, local_target), "tensor"
    )
    lse = row_peak + jnp.log(row_total)
    row_logprob = target_logit - lse
    row_entropy = lse - row_weighted / row_total
    own_first = lax.axis_index("tensor") * own_rows
    positions = own_first + jnp.arange(own_rows, dtype=jnp.int32)
    matches = order_all[None, :] == positions[:, None]
    logprob = jnp.sum(jnp.where(matches, row_logprob[None, :], 0.0), axis=1)
    entropy = jnp.sum(jnp.where(matches, row_entropy[None, :], 0.0), axis=1)
    starts = jnp.cumsum(lengths) - lengths
    member = (positions[:, None] >= starts[None, :]) & (
        positions[:, None] < (starts + lengths)[None, :]
    )
    part_logprob = jnp.sum(jnp.where(member, logprob[:, None], 0.0), axis=0)
    part_entropy = jnp.sum(jnp.where(member, entropy[:, None], 0.0), axis=0)
    sum_logprob, sum_entropy = lax.psum((part_logprob, part_entropy), "tensor")
    counts = lengths.astype(jnp.float32)
    return (logprob, entropy, sum_logprob / counts, sum_entropy / counts)


def solution(mesh):
    return jax.shard_map(
        per_device,
        mesh=mesh,
        in_specs=(
            P(("dp", "tensor"), None),
            P(),
            P(None, "tensor"),
            P(("dp", "tensor")),
            P(("dp", "tensor")),
            P("dp"),
        ),
        out_specs=(P(("dp", "tensor")), P(("dp", "tensor")), P("dp"), P("dp")),
        check_vma=False,
    )
```

profile of v0, /device:TPU:10, one launch (start us, length us, event | category | flops | bytes accessed | tf_op | source)
XLA Modules:
  0.0 1031.8 jit_solution(12010160230439530496)
XLA Ops:
  7.2 0.0 copy-start
  7.2 0.0 copy-start.3
  7.2 0.0 all-gather.2.cloned.1.call-start
  7.2 0.8 convert_element_type.13
  8.1 1.0 fusion.3
  9.1 1.7 fusion.5
  10.8 0.0 all-gather.2.cloned.1.call-update
  10.9 1.3 dynamic-slice
  12.8 0.9 dynamic-update-slice.1
  13.7 0.9 dynamic-update-slice
  14.5 282.0 %all-reduce.2 = (s32[3072]{0:T(1024)S(1)}, s32[3072]{0:T(1024)S(1)}) all-reduce(s32[3072]{0:T(1024)S(1)} %dynamic-update-slice.1, s32[3072]{0:T(1024)S(1)} %dynamic-update-slice), channel_id=1, replica_groups=mesh['dp'=8,'tensor'=64] {'tensor'}, use_global_device_ids=true, to_apply=%add.1 | all-reduce | flops 6144 | bytes 49152
  296.5 17.4 %gather_fusion = s32[3072]{0:T(1024)S(1)} fusion(s32[3072]{0:T(1024)S(1)} %get-tuple-element.11, s32[3072]{0:T(1024)S(1)} %fusion.6), kind=kCustom, calls=%fused_computation | custom fusion | bytes 36864 | tf_op jit(solution)/shard_map/gather | solution.py:21
  313.9 0.0 copy-done.3
  313.9 0.2 reduce-window.8
  314.1 0.0 all-gather.2.cloned.1.call-done
  314.1 0.0 copy-done
  314.2 12.4 %fusion.8 = (f32[3072]{0:T(1024)S(1)}, f32[3072,768]{0,1:T(8,128)}) fusion(bf16[3072,1536]{1,0:T(8,128)(2,1)} %all-gather.2.cloned.1.call-done, bf16[1536,768]{1,0:T(8,128)(2,1)S(1)} %copy-done), kind=kOutput, calls=%fused_computation.29 | convolution fusion | flops 7250113536 | bytes 21245952 | tf_op jit(solution)/shard_map/dot_general | solution.py:24
  326.5 276.2 %pmax.7 = f32[3072]{0:T(1024)S(1)} all-reduce(f32[3072]{0:T(1024)S(1)} %get-tuple-element.22), channel_id=1, replica_groups=mesh['dp'=8,'tensor'=64] {'tensor'}, use_global_device_ids=true, to_apply=%region_4.0 | all-reduce | flops 3072 | bytes 24576 | tf_op jit(solution)/shard_map/pmax | solution.py:30
  602.7 5.8 multiply_reduce_fusion
  608.6 274.1 %all-reduce.4 = (f32[3072]{0:T(1024)S(1)}, f32[3072]{0:T(1024)S(1)}, f32[3072]{0:T(1024)S(1)}) all-reduce(f32[3072]{0:T(1024)S(1)} %get-tuple-element.4, f32[3072]{0:T(1024)S(1)} %get-tuple-element.5, f32[3072]{0:T(1024)S(1)} %get-tuple-element.6), channel_id=1, replica_groups=mesh['dp'=8,'tensor'=64] {'tensor'}, use_global_device_ids=true, to_apply=%region_9.10 | all-reduce | flops 9216 | bytes 73728 | tf_op jit(solution)/shard_map/psum | solution.py:35
  882.7 0.3 fusion.2
  883.0 0.0 copy-start.1
  883.0 0.0 copy-start.2
  883.0 0.2 select_reduce_fusion.1
  883.2 141.2 %all-reduce.3 = (f32[8]{0:T(128)S(1)}, f32[8]{0:T(128)S(1)}) all-reduce(f32[8]{0:T(128)S(1)} %get-tuple-element.10, f32[8]{0:T(128)S(1)} %get-tuple-element.9), channel_id=1, replica_groups=mesh['dp'=8,'tensor'=64] {'tensor'}, use_global_device_ids=true, to_apply=%region_13.14 | all-reduce | flops 16 | bytes 128 | tf_op jit(solution)/shard_map/psum | solution.py:52
  1024.5 0.5 convert_divide_fusion
  1025.0 0.0 copy-done.1
  1025.0 0.0 copy-done.2
  (8 shorter events, 0.0 us)
Async XLA Ops:
  7.2 307.0 %copy-start = (bf16[1536,768]{1,0:T(8,128)(2,1)S(1)}, bf16[1536,768]{1,0:T(8,128)(2,1)}, u32[]{:S(2)}) copy-start(bf16[1536,768]{1,0:T(8,128)(2,1)} %param.8) | copy-start | bytes 7077892
  7.2 306.7 %copy-start.3 = (s32[8]{0:T(128)S(1)}, s32[8]{0:T(128)}, u32[]{:S(2)}) copy-start(s32[8]{0:T(128)} %param.11) | copy-start | bytes 100
  7.2 306.9 %all-gather.2.cloned.1.call-start = ((), (), s32[]{:S(2)}) async-start(), calls=%async_computation | async-start | bytes 9584640 | tf_op jit(solution)/shard_map/all_gather | solution.py:25
  883.0 142.0 %copy-start.1 = (f32[48]{0:T(128)}, f32[48]{0:T(128)S(1)}, u32[]{:S(2)}) copy-start(f32[48]{0:T(128)S(1)} %get-tuple-element.7) | copy-start | bytes 580
  883.0 142.0 %copy-start.2 = (f32[48]{0:T(128)}, f32[48]{0:T(128)S(1)}, u32[]{:S(2)}) copy-start(f32[48]{0:T(128)S(1)} %get-tuple-element.8) | copy-start | bytes 580
Sparse Core Ops, SparseCore 0:
  11.0 162.6 all-gather.1
where the time goes:
time: 1030 us
  blocking collectives  974 us (95%)
  local copies, waits for them, and re-layouts  20.4 us (2%)
  between operations  14.8 us (1%)
  matrix products  12.4 us (1%)
  other arithmetic  10.7 us (1%)
    unnamed x1, blocking collectives  282 us
    pmax x1, blocking collectives, per_device(): row_peak = lax.pmax(local_peak, 'tensor')  276 us
    psum x1, blocking collectives, per_device(): lax.psum((local_total, local_weighted, local_target), 'tensor')  274 us
    psum x1, blocking collectives, per_device(): sum_logprob, sum_entropy = lax.psum((part_logprob, part_entropy), 'tensor')  141 us
  transfers between devices with their start and end apart: 1, of which 0 were waited for; matrix products, arithmetic and copies ran while one was open for 2% of the time, Pallas kernels for 0%

commit v1 on v0

v1 whole, which is shorter than its diff:
```python
import functools

import jax
import jax.numpy as jnp
from jax import lax
from jax.experimental import pallas as pl
from jax.experimental.pallas import tpu as pltpu
from jax.sharding import PartitionSpec as P

MESH = pl.DeviceIdType.MESH
NX, NY, NZ = 4, 4, 16
NT = NZ * NY
CHUNK = 256
OFFSETS = (NY - 1, 1, 2, 0)


def kernel(
    hid, gain, w_hbm, meta_in, lengths, out,
    xs, wb, lg, meta, thi, tlo, mx, sm, wt, st, stg, fing, fin,
    own_sem, tok_s, tok_r, met_s, met_r, my_s, my_r, wy_s, wy_r, wx_s, wx_r, wp_s, wp_r, b_s, b_r, c_s, c_r,
):
    rows, width = hid.shape
    depth, cols = w_hbm.shape
    per_slice = cols // CHUNK
    seqs = lengths.shape[0]
    dp, tt = lax.axis_index("dp"), lax.axis_index("tensor")
    core, x = lax.rem(dp, 2), lax.div(dp, 2)
    y, z = lax.rem(tt, NY), lax.div(tt, NY)
    q = lax.rem(x, 2)

    def dev(dx=0, dy=0, dz=0, other=False):
        c = 1 - core if other else core
        return (
            lax.rem(x + dx + NX, NX) * 2 + c,
            lax.rem(z + dz + NZ, NZ) * NY + lax.rem(y + dy + NY, NY),
        )

    def send(src, dst, ssem, rsem, device):
        copy = pltpu.make_async_remote_copy(
            src_ref=src, dst_ref=dst, send_sem=ssem, recv_sem=rsem, device_id=device, device_id_type=MESH
        )
        copy.start()
        sent.append(copy)
        return copy

    sent = []
    barrier = pltpu.get_barrier_semaphore()
    friends = [dev(dy=1), dev(dy=-1), dev(dy=2), dev(dz=1), dev(dz=-1), dev(dx=1), dev(dx=-1), dev(other=True)]
    for friend in friends:
        pl.semaphore_signal(barrier, inc=1, device_id=friend, device_id_type=MESH)
    own_copy = pltpu.make_async_copy(w_hbm, wb.at[3], own_sem)
    own_copy.start()
    meta[tt] = meta_in[...]
    values = hid[...].astype(jnp.float32)
    scale = lax.rsqrt(jnp.mean(values * values, axis=-1, keepdims=True) + 1e-05)
    xs[0:rows, :] = (values * scale * gain[...].astype(jnp.float32)).astype(jnp.bfloat16)
    mx[...] = jnp.full(mx.shape, -jnp.inf, jnp.float32)
    sm[...] = jnp.zeros_like(sm)
    wt[...] = jnp.zeros_like(wt)
    thi[...] = jnp.zeros_like(thi)
    tlo[...] = jnp.zeros_like(tlo)
    pl.semaphore_wait(barrier, len(friends))

    def slot(s):
        return xs.at[pl.ds(s * rows, rows), :]

    def send_tokens(k):
        right = send(slot(max(2 * k - 3, 0)), slot(2 * k - 1), tok_s.at[0, k - 1], tok_r.at[0, k - 1], dev(dz=1))
        left = None
        if k < NZ // 2:
            left = send(slot(2 * k - 2), slot(2 * k), tok_s.at[1, k - 1], tok_r.at[1, k - 1], dev(dz=-1))
        return right, left

    def send_meta(k):
        there = meta.at[pl.ds(lax.rem(z - (k - 1) + NZ, NZ) * NY, NY)]
        right = send(there, there, met_s.at[0, k - 1], met_r.at[0, k - 1], dev(dz=1))
        left = None
        if k < NZ // 2:
            there = meta.at[pl.ds(lax.rem(z + (k - 1), NZ) * NY, NY)]
            left = send(there, there, met_s.at[1, k - 1], met_r.at[1, k - 1], dev(dz=-1))
        return right, left

    def row_at(c, parity, e):
        quarter = depth // 4
        return pl.multiple_of(c * (depth // 2) + parity * quarter + e * (quarter // 2), 64)

    def part(r, c, parity, e):
        return wb.at[r, pl.ds(row_at(c, parity, e), depth // 8), :]

    def mine(e):
        return w_hbm.at[pl.ds(row_at(core, q, e), depth // 8), :]

    wy, wx, wp = {}, {}, {}

    def send_y(r, e, src, dy):
        wy[r, e] = send(src, part(r, core, q, e), wy_s.at[r, e], wy_r.at[r, e], dev(dy=dy))

    def got_y(r, e):
        wy[r, e].wait_recv()
        here = part(r, core, q, e)
        if (r, e) == (0, 0):
            send_y(2, 0, here, 1)
        if (r, e) == (1, 1):
            send_y(2, 1, here, -1)
        wx[r, e] = send(here, here, wx_s.at[r, e], wx_r.at[r, e], dev(dx=1 if e == 0 else -1))
        wp[0, r, e] = send(here, here, wp_s.at[0, r, e], wp_r.at[0, r, e], dev(other=True))

    def got_x(r, e):
        wx[r, e].wait_recv()
        here = part(r, core, 1 - q, e)
        wp[1, r, e] = send(here, here, wp_s.at[1, r, e], wp_r.at[1, r, e], dev(other=True))

    def got_partner(r):
        for source in (0, 1):
            for e in (0, 1):
                wp[source, r, e].wait_recv()

    def job(first, count, r_first, r_count):
        here = pl.ds(first, count)

        def step(i, carry):
            j = r_first * per_slice + i
            r, c = lax.div(j, per_slice), lax.rem(j, per_slice)
            block = wb[r, :, pl.ds(pl.multiple_of(c * CHUNK, CHUNK), CHUNK)]
            logits = jnp.dot(xs[here, :], block, preferred_element_type=jnp.float32)
            lg[j, here, :] = logits
            old = mx[here, :]
            peak = jnp.maximum(old, jnp.max(logits, axis=-1, keepdims=True))
            fade = jnp.exp(old - peak)
            exponent = jnp.exp(logits - peak)
            mx[here, :] = peak
            sm[here, :] = sm[here, :] * fade + jnp.sum(exponent, axis=-1, keepdims=True)
            wt[here, :] = wt[here, :] * fade + jnp.sum(exponent * logits, axis=-1, keepdims=True)
            return carry

        lax.fori_loop(0, r_count * per_slice, step, 0)

    tokens = {1: send_tokens(1)}
    metas = {}
    meta_y = [
        send(meta.at[tt], meta.at[tt], my_s.at[i], my_r.at[i], dev(dy=dy)) for i, dy in enumerate((1, -1, 2))
    ]
    send_y(0, 0, mine(0), 1)
    send_y(1, 1, mine(1), -1)
    send_y(0, 1, mine(1), 1)
    send_y(1, 0, mine(0), -1)
    for copy in meta_y:
        copy.wait_recv()
    metas[1] = send_meta(1)

    def ring(k):
        for pair, start in ((tokens, send_tokens), (metas, send_meta)):
            for copy in pair[k]:
                if copy is not None:
                    copy.wait_recv()
            if k < NZ // 2:
                pair[k + 1] = start(k + 1)

    near, mid = 5 * rows, 11 * rows
    total_rows = NZ * rows
    ring(1)
    got_y(0, 0)
    got_y(1, 1)
    ring(2)
    own_copy.wait()
    job(0, near, 3, 1)
    ring(3)
    got_y(0, 1)
    got_y(1, 0)
    got_x(0, 0)
    got_x(1, 1)
    ring(4)
    ring(5)
    job(near, mid - near, 3, 1)
    got_y(2, 0)
    got_y(2, 1)
    got_x(0, 1)
    got_x(1, 0)
    ring(6)
    got_partner(0)
    got_partner(1)
    job(0, mid, 0, 2)
    ring(7)
    got_x(2, 0)
    got_x(2, 1)
    got_partner(2)
    job(0, mid, 2, 1)
    ring(8)
    job(mid, total_rows - mid, 0, 4)

    lane = lax.broadcasted_iota(jnp.int32, (rows, 128), 1)
    eye = lane == lax.broadcasted_iota(jnp.int32, (rows, 128), 0)
    for t in range(NT):
        ids = meta[t, 1:2, :]
        high = ids >> 8
        thi[t:t + 1, :] = high.astype(jnp.float32)
        tlo[t:t + 1, :] = (ids - (high << 8)).astype(jnp.float32)
    high_ids, low_ids = thi[...].astype(jnp.bfloat16), tlo[...].astype(jnp.bfloat16)
    lane_chunk = lax.broadcasted_iota(jnp.int32, (rows, CHUNK), 1)

    def to_row(column):
        return jnp.sum(jnp.where(eye, column, 0.0), axis=0, keepdims=True)

    stats = []

    def send_stats(s):
        k = (s + 1) // 2
        if s % 2:
            theirs, dz = (2 * k if k < NZ // 2 else s), -k
        else:
            theirs, dz = 2 * k - 1, k
        stats.append(send(st.at[s], stg.at[theirs], b_s.at[s], b_r.at[theirs], dev(dz=dz)))

    for s in range(NZ - 1, -1, -1):
        k = (s + 1) // 2
        zs = lax.rem(z + (-k if s % 2 else k) + NZ, NZ)
        order = meta[zs * NY + y, 0:1, :]
        order = jnp.sum(jnp.where(eye, order.astype(jnp.float32), 0.0), axis=1, keepdims=True).astype(jnp.int32)
        inside = (order >= lane * rows) & (order < lane * rows + rows)
        picked = jnp.where(inside, 1.0, 0.0).astype(jnp.bfloat16)
        ids = 256.0 * jnp.dot(picked, high_ids, preferred_element_type=jnp.float32) + jnp.dot(
            picked, low_ids, preferred_element_type=jnp.float32
        )
        start = jnp.sum(jnp.where(inside, (lane * rows).astype(jnp.float32), 0.0), axis=1, keepdims=True)
        wanted = jnp.sum(
            jnp.where(lane == order - start.astype(jnp.int32), ids, 0.0), axis=1, keepdims=True
        ).astype(jnp.int32)
        found = jnp.zeros((rows, CHUNK), jnp.float32)
        for j in range(4 * per_slice):
            base = (z * NY + lax.rem(y + OFFSETS[j // per_slice], NY)) * cols + (j % per_slice) * CHUNK
            found += jnp.where(lane_chunk == wanted - base, lg[j, s * rows:(s + 1) * rows, :], 0.0)
        target = jnp.sum(found, axis=-1, keepdims=True)
        here = slice(s * rows, (s + 1) * rows)
        place = stg if s == 0 else st
        place[s, 0:1, :] = to_row(mx[here, :])
        place[s, 1:2, :] = to_row(sm[here, :])
        place[s, 2:3, :] = to_row(wt[here, :])
        place[s, 3:4, :] = to_row(target)
        if s + 1 < NZ:
            send_stats(s + 1)

    for copy in stats:
        copy.wait_recv()
    peak = stg[0, 0:1, :]
    for s in range(1, NZ):
        peak = jnp.maximum(peak, stg[s, 0:1, :])
    row_total = jnp.zeros((1, 128), jnp.float32)
    row_weighted, target_logit = row_total, row_total
    for s in range(NZ):
        fade = jnp.exp(stg[s, 0:1, :] - peak)
        row_total += stg[s, 1:2, :] * fade
        row_weighted += stg[s, 2:3, :] * fade
        target_logit += stg[s, 3:4, :]
    row_total = jnp.where(lane[0:1, :] < rows, row_total, 1.0)
    lse = peak + jnp.log(row_total)
    fing[0:1, :] = target_logit - lse
    fing[1:2, :] = lse - row_weighted / row_total
    fin[tt] = fing[...]

    def final_copy(i):
        other = lax.rem(tt + i, NT)
        return pltpu.make_async_remote_copy(
            src_ref=fing, dst_ref=fin.at[tt], send_sem=c_s.at[i], recv_sem=c_r.at[i],
            device_id=(dp, other), device_id_type=MESH,
        )

    def start_final(i, carry):
        final_copy(i).start()
        return carry

    lax.fori_loop(1, NT, start_final, 0)
    sub8 = lax.broadcasted_iota(jnp.int32, (seqs, 128), 0)
    lane8 = lax.broadcasted_iota(jnp.int32, (seqs, 128), 1)
    first = jnp.zeros((seqs, 128), jnp.int32)
    last = first
    running = jnp.int32(0)
    for i in range(seqs):
        first = jnp.where(sub8 == i, running, first)
        running = running + lengths[i]
        last = jnp.where(sub8 == i, running, last)
    for copy in sent:
        copy.wait_send()

    def end_final(i, carry):
        final_copy(i).wait()
        return carry

    lax.fori_loop(1, NT, end_final, 0)
    position = tt * rows + lax.broadcasted_iota(jnp.int32, (rows, 128), 0)

    def place_rows(t, carry):
        logprob, entropy, seq_logprob, seq_entropy = carry
        order = meta[t, 0:1, :]
        got_logprob, got_entropy = fin[t, 0:1, :], fin[t, 1:2, :]
        match = order == position
        member = (order >= first) & (order < last)
        return (
            logprob + jnp.where(match, got_logprob, 0.0),
            entropy + jnp.where(match, got_entropy, 0.0),
            seq_logprob + jnp.where(member, got_logprob, 0.0),
            seq_entropy + jnp.where(member, got_entropy, 0.0),
        )

    wide, narrow = jnp.zeros((rows, 128), jnp.float32), jnp.zeros((seqs, 128), jnp.float32)
    logprob, entropy, seq_logprob, seq_entropy = lax.fori_loop(0, NT, place_rows, (wide, wide, narrow, narrow))
    out[...] = jnp.zeros_like(out)
    out[0:1, :] = to_row(jnp.sum(logprob, axis=1, keepdims=True))
    out[1:2, :] = to_row(jnp.sum(entropy, axis=1, keepdims=True))
    counts = (last - first).astype(jnp.float32)
    for i, value in ((2, seq_logprob), (3, seq_entropy)):
        mean = jnp.sum(value, axis=1, keepdims=True) / counts
        out[i:i + 1, :] = jnp.sum(jnp.where(sub8 == lane8, mean, 0.0), axis=0, keepdims=True)


def per_device(hidden, norm_gain, head_weight, token_order, targets, lengths):
    rows, width = hidden.shape
    depth, cols = head_weight.shape
    seqs = lengths.shape[0]
    meta = jnp.stack([
        jnp.pad(token_order, (0, 128 - rows), constant_values=-1),
        jnp.pad(targets, (0, 128 - rows)),
    ])
    total = NZ * rows
    vmem, dma = pltpu.VMEM, pltpu.SemaphoreType.DMA
    half = NZ // 2
    in_vmem = pl.BlockSpec(memory_space=pltpu.VMEM)
    out = pl.pallas_call(
        kernel,
        out_shape=jax.ShapeDtypeStruct((8, 128), jnp.float32),
        in_specs=[
            in_vmem, in_vmem, pl.BlockSpec(memory_space=pl.ANY), in_vmem, pl.BlockSpec(memory_space=pltpu.SMEM),
        ],
        out_specs=in_vmem,
        scratch_shapes=[
            vmem((total, width), jnp.bfloat16),
            vmem((4, depth, cols), jnp.bfloat16),
            vmem((4 * cols // CHUNK, total, CHUNK), jnp.float32),
            vmem((NT, 2, 128), jnp.int32),
            vmem((128, 128), jnp.float32),
            vmem((128, 128), jnp.float32),
            vmem((total, 1), jnp.float32),
            vmem((total, 1), jnp.float32),
            vmem((total, 1), jnp.float32),
            vmem((NZ, 4, 128), jnp.float32),
            vmem((NZ, 4, 128), jnp.float32),
            vmem((2, 128), jnp.float32),
            vmem((NT, 2, 128), jnp.float32),
            dma,
            dma((2, half)), dma((2, half)),
            dma((2, half)), dma((2, half)),
            dma((3,)), dma((3,)),
            dma((3, 2)), dma((3, 2)),
            dma((3, 2)), dma((3, 2)),
            dma((2, 3, 2)), dma((2, 3, 2)),
            dma((NZ,)), dma((NZ,)),
            dma((NT,)), dma((NT,)),
        ],
        compiler_params=pltpu.CompilerParams(
            collective_id=0, has_side_effects=True, vmem_limit_bytes=60 * 1024 * 1024
        ),
    )(hidden, norm_gain.reshape(1, width), head_weight, meta, lengths)
    return out[0, :rows], out[1, :rows], out[2, :seqs], out[3, :seqs]


def solution(mesh):
    return jax.shard_map(
        per_device,
        mesh=mesh,
        in_specs=(
            P(("dp", "tensor"), None),
            P(),
            P(None, "tensor"),
            P(("dp", "tensor")),
            P(("dp", "tensor")),
            P("dp"),
        ),
        out_specs=(P(("dp", "tensor")), P(("dp", "tensor")), P("dp"), P("dp")),
        check_vma=False,
    )
```

time: 1030 us -> 97.5 us (0.09)
  the two profiles are of different devices: /device:TPU:10 before, /device:TPU:1 now
where the time goes in v1:
time: 97.5 us; the launch traced here: 97.2 us
  Pallas kernels  91.5 us (94%)
  local copies, waits for them, and re-layouts  4.49 us (5%)
    pallas_call x1, Pallas kernels, per_device(): pl.pallas_call(kernel, out_shape=jax.ShapeDtypeStruct((8, 128), jnp.float...  91.5 us
    squeeze x2, local copies, waits for them, and re-layouts, per_device(): return (out[0, :rows], out[1, :rows], out[2, :seqs], out[3, :seqs])  2.53 us

profile of v1, /device:TPU:1, one launch (start us, length us, event | category | flops | bytes accessed | tf_op | source)
XLA Modules:
  0.0 97.2 jit_solution(12450629891014134086)
XLA Ops:
  0.6 0.7 pad_bitcast_fusion
  1.3 0.6 pad_add_fusion.meta_in
  1.9 1.3 %reshape.11.gain = bf16[1,1536]{1,0:T(2,128)(2,1)} reshape(bf16[1536]{0:T(1024)(128)(2,1)} %param.7) | data formatting | bytes 6144 | tf_op jit(solution)/shard_map/reshape | solution.py:361
  3.1 91.5 %shard_map.93 = f32[8,128]{1,0:T(8,128)} custom-call(bf16[48,1536]{1,0:T(8,128)(2,1)} %hid.1, bf16[1,1536]{1,0:T(2,128)(2,1)} %reshape.11.gain, bf16[1536,768]{1,0:T(8,128)(2,1)} %w_hbm.1, s32[2,128]{1,0:T(2,128)} %pad_add_fusion.meta_in, s32[8]{0:T(128)} %lengths.1), custom_call_target="tpu_custom_call" | custom-call | tf_op jit(solution)/shard_map/pallas_call | solution.py:327
  94.7 1.3 %slice_bitcast_fusion.2 = (f32[48]{0:T(128)}, f32[48]{0:T(128)}) fusion(f32[8,128]{1,0:T(8,128)} %shard_map.93), kind=kLoop, calls=%fused_computation.3 | loop fusion | bytes 768 | tf_op jit(solution)/shard_map/squeeze | solution.py:362
  96.0 1.3 %slice_bitcast_fusion = (f32[8]{0:T(128)}, f32[8]{0:T(128)}) fusion(f32[8,128]{1,0:T(8,128)} %shard_map.93), kind=kLoop, calls=%fused_computation.1 | loop fusion | bytes 128 | tf_op jit(solution)/shard_map/squeeze | solution.py:362

commit v2 on v1

--- a/solution.py
+++ b/solution.py
@@ -10,18 +10,17 @@
 MESH = pl.DeviceIdType.MESH
 NX, NY, NZ = 4, 4, 16
 NT = NZ * NY
-CHUNK = 256
+PIECE = 16
 OFFSETS = (NY - 1, 1, 2, 0)
 
 
 def kernel(
-    hid, gain, w_hbm, meta_in, lengths, out,
+    hid, gain, w_hbm, order_in, target_in, lengths, out_logprob, out_entropy, out_seq_logprob, out_seq_entropy,
     xs, wb, lg, meta, thi, tlo, mx, sm, wt, st, stg, fing, fin,
     own_sem, tok_s, tok_r, met_s, met_r, my_s, my_r, wy_s, wy_r, wx_s, wx_r, wp_s, wp_r, b_s, b_r, c_s, c_r,
 ):
     rows, width = hid.shape
     depth, cols = w_hbm.shape
-    per_slice = cols // CHUNK
     seqs = lengths.shape[0]
     dp, tt = lax.axis_index("dp"), lax.axis_index("tensor")
     core, x = lax.rem(dp, 2), lax.div(dp, 2)
@@ -50,10 +49,13 @@
         pl.semaphore_signal(barrier, inc=1, device_id=friend, device_id_type=MESH)
     own_copy = pltpu.make_async_copy(w_hbm, wb.at[3], own_sem)
     own_copy.start()
-    meta[tt] = meta_in[...]
+    meta[tt, 0:1, :] = jnp.full((1, 128), -1, jnp.int32)
+    meta[tt, 1:2, :] = jnp.zeros((1, 128), jnp.int32)
+    meta[tt, 0:1, 0:rows] = order_in[...].reshape(1, rows)
+    meta[tt, 1:2, 0:rows] = target_in[...].reshape(1, rows)
     values = hid[...].astype(jnp.float32)
     scale = lax.rsqrt(jnp.mean(values * values, axis=-1, keepdims=True) + 1e-05)
-    xs[0:rows, :] = (values * scale * gain[...].astype(jnp.float32)).astype(jnp.bfloat16)
+    xs[0:rows, :] = (values * scale * gain[...].astype(jnp.float32).reshape(1, width)).astype(jnp.bfloat16)
     mx[...] = jnp.full(mx.shape, -jnp.inf, jnp.float32)
     sm[...] = jnp.zeros_like(sm)
     wt[...] = jnp.zeros_like(wt)
@@ -61,15 +63,16 @@
     tlo[...] = jnp.zeros_like(tlo)
     pl.semaphore_wait(barrier, len(friends))
 
-    def slot(s):
-        return xs.at[pl.ds(s * rows, rows), :]
-
-    def send_tokens(k):
-        right = send(slot(max(2 * k - 3, 0)), slot(2 * k - 1), tok_s.at[0, k - 1], tok_r.at[0, k - 1], dev(dz=1))
-        left = None
-        if k < NZ // 2:
-            left = send(slot(2 * k - 2), slot(2 * k), tok_s.at[1, k - 1], tok_r.at[1, k - 1], dev(dz=-1))
-        return right, left
+    def slot(s, piece):
+        return xs.at[pl.ds(s * rows + piece * PIECE, PIECE), :]
+
+    def send_tokens(k, piece):
+        def one(way, source, target, dz):
+            where = way, k - 1, piece
+            return send(slot(source, piece), slot(target, piece), tok_s.at[where], tok_r.at[where], dev(dz=dz))
+
+        right = one(0, max(2 * k - 3, 0), 2 * k - 1, 1)
+        return (right, one(1, 2 * k - 2, 2 * k, -1)) if k < NZ // 2 else (right,)
 
     def send_meta(k):
         there = meta.at[pl.ds(lax.rem(z - (k - 1) + NZ, NZ) * NY, NY)]
@@ -119,23 +122,25 @@
         here = pl.ds(first, count)
 
         def step(i, carry):
-            j = r_first * per_slice + i
-            r, c = lax.div(j, per_slice), lax.rem(j, per_slice)
-            block = wb[r, :, pl.ds(pl.multiple_of(c * CHUNK, CHUNK), CHUNK)]
-            logits = jnp.dot(xs[here, :], block, preferred_element_type=jnp.float32)
-            lg[j, here, :] = logits
+            r = r_first + i
+            logits = jnp.dot(xs[here, :], wb[r], preferred_element_type=jnp.float32)
+            parts = [logits[:, c:c + 128] for c in range(0, cols, 128)]
+            lg[r, here, :] = logits
             old = mx[here, :]
-            peak = jnp.maximum(old, jnp.max(logits, axis=-1, keepdims=True))
+            peak = functools.reduce(jnp.maximum, parts, old)
             fade = jnp.exp(old - peak)
-            exponent = jnp.exp(logits - peak)
-            mx[here, :] = peak
-            sm[here, :] = sm[here, :] * fade + jnp.sum(exponent, axis=-1, keepdims=True)
-            wt[here, :] = wt[here, :] * fade + jnp.sum(exponent * logits, axis=-1, keepdims=True)
+            total, weighted = sm[here, :] * fade, wt[here, :] * fade
+            for piece in parts:
+                exponent = jnp.exp(piece - peak)
+                total += exponent
+                weighted += exponent * piece
+            mx[here, :], sm[here, :], wt[here, :] = peak, total, weighted
             return carry
 
-        lax.fori_loop(0, r_count * per_slice, step, 0)
-
-    tokens = {1: send_tokens(1)}
+        lax.fori_loop(0, r_count, step, 0)
+
+    pieces = rows // PIECE
+    tokens = {(1, piece): send_tokens(1, piece) for piece in range(pieces)}
     metas = {}
     meta_y = [
         send(meta.at[tt], meta.at[tt], my_s.at[i], my_r.at[i], dev(dy=dy)) for i, dy in enumerate((1, -1, 2))
@@ -149,12 +154,16 @@
     metas[1] = send_meta(1)
 
     def ring(k):
-        for pair, start in ((tokens, send_tokens), (metas, send_meta)):
-            for copy in pair[k]:
-                if copy is not None:
-                    copy.wait_recv()
+        for copy in metas[k]:
+            if copy is not None:
+                copy.wait_recv()
+        if k < NZ // 2:
+            metas[k + 1] = send_meta(k + 1)
+        for piece in range(pieces):
+            for copy in tokens[k, piece]:
+                copy.wait_recv()
             if k < NZ // 2:
-                pair[k + 1] = start(k + 1)
+                tokens[k + 1, piece] = send_tokens(k + 1, piece)
 
     near, mid = 5 * rows, 11 * rows
     total_rows = NZ * rows
@@ -196,7 +205,6 @@
         thi[t:t + 1, :] = high.astype(jnp.float32)
         tlo[t:t + 1, :] = (ids - (high << 8)).astype(jnp.float32)
     high_ids, low_ids = thi[...].astype(jnp.bfloat16), tlo[...].astype(jnp.bfloat16)
-    lane_chunk = lax.broadcasted_iota(jnp.int32, (rows, CHUNK), 1)
 
     def to_row(column):
         return jnp.sum(jnp.where(eye, column, 0.0), axis=0, keepdims=True)
@@ -225,16 +233,20 @@
         wanted = jnp.sum(
             jnp.where(lane == order - start.astype(jnp.int32), ids, 0.0), axis=1, keepdims=True
         ).astype(jnp.int32)
-        found = jnp.zeros((rows, CHUNK), jnp.float32)
-        for j in range(4 * per_slice):
-            base = (z * NY + lax.rem(y + OFFSETS[j // per_slice], NY)) * cols + (j % per_slice) * CHUNK
-            found += jnp.where(lane_chunk == wanted - base, lg[j, s * rows:(s + 1) * rows, :], 0.0)
+        here = slice(s * rows, (s + 1) * rows)
+        found = jnp.zeros((rows, 128), jnp.float32)
+        for r in range(4):
+            near_wanted = wanted - (z * NY + lax.rem(y + OFFSETS[r], NY)) * cols
+            for c in range(0, cols, 128):
+                found += jnp.where(lane == near_wanted - c, lg[r, here, c:c + 128], 0.0)
         target = jnp.sum(found, axis=-1, keepdims=True)
-        here = slice(s * rows, (s + 1) * rows)
+        lane_peak = mx[here, :]
+        peak = jnp.max(lane_peak, axis=-1, keepdims=True)
+        fade = jnp.exp(lane_peak - peak)
         place = stg if s == 0 else st
-        place[s, 0:1, :] = to_row(mx[here, :])
-        place[s, 1:2, :] = to_row(sm[here, :])
-        place[s, 2:3, :] = to_row(wt[here, :])
+        place[s, 0:1, :] = to_row(peak)
+        place[s, 1:2, :] = to_row(jnp.sum(sm[here, :] * fade, axis=-1, keepdims=True))
+        place[s, 2:3, :] = to_row(jnp.sum(wt[here, :] * fade, axis=-1, keepdims=True))
         place[s, 3:4, :] = to_row(target)
         if s + 1 < NZ:
             send_stats(s + 1)
@@ -303,50 +315,46 @@
 
     wide, narrow = jnp.zeros((rows, 128), jnp.float32), jnp.zeros((seqs, 128), jnp.float32)
     logprob, entropy, seq_logprob, seq_entropy = lax.fori_loop(0, NT, place_rows, (wide, wide, narrow, narrow))
-    out[...] = jnp.zeros_like(out)
-    out[0:1, :] = to_row(jnp.sum(logprob, axis=1, keepdims=True))
-    out[1:2, :] = to_row(jnp.sum(entropy, axis=1, keepdims=True))
+    out_logprob[...] = to_row(jnp.sum(logprob, axis=1, keepdims=True))[0, :rows]
+    out_entropy[...] = to_row(jnp.sum(entropy, axis=1, keepdims=True))[0, :rows]
     counts = (last - first).astype(jnp.float32)
-    for i, value in ((2, seq_logprob), (3, seq_entropy)):
+    for ref, value in ((out_seq_logprob, seq_logprob), (out_seq_entropy, seq_entropy)):
         mean = jnp.sum(value, axis=1, keepdims=True) / counts
-        out[i:i + 1, :] = jnp.sum(jnp.where(sub8 == lane8, mean, 0.0), axis=0, keepdims=True)
+        ref[...] = jnp.sum(jnp.where(sub8 == lane8, mean, 0.0), axis=0, keepdims=True)[0, :seqs]
 
 
 def per_device(hidden, norm_gain, head_weight, token_order, targets, lengths):
     rows, width = hidden.shape
     depth, cols = head_weight.shape
     seqs = lengths.shape[0]
-    meta = jnp.stack([
-        jnp.pad(token_order, (0, 128 - rows), constant_values=-1),
-        jnp.pad(targets, (0, 128 - rows)),
-    ])
     total = NZ * rows
     vmem, dma = pltpu.VMEM, pltpu.SemaphoreType.DMA
     half = NZ // 2
     in_vmem = pl.BlockSpec(memory_space=pltpu.VMEM)
-    out = pl.pallas_call(
+    return pl.pallas_call(
         kernel,
-        out_shape=jax.ShapeDtypeStruct((8, 128), jnp.float32),
+        out_shape=[jax.ShapeDtypeStruct((n,), jnp.float32) for n in (rows, rows, seqs, seqs)],
         in_specs=[
-            in_vmem, in_vmem, pl.BlockSpec(memory_space=pl.ANY), in_vmem, pl.BlockSpec(memory_space=pltpu.SMEM),
+            in_vmem, in_vmem, pl.BlockSpec(memory_space=pl.ANY), in_vmem, in_vmem,
+            pl.BlockSpec(memory_space=pltpu.SMEM),
         ],
-        out_specs=in_vmem,
+        out_specs=[in_vmem] * 4,
         scratch_shapes=[
             vmem((total, width), jnp.bfloat16),
             vmem((4, depth, cols), jnp.bfloat16),
-            vmem((4 * cols // CHUNK, total, CHUNK), jnp.float32),
+            vmem((4, total, cols), jnp.float32),
             vmem((NT, 2, 128), jnp.int32),
             vmem((128, 128), jnp.float32),
             vmem((128, 128), jnp.float32),
-            vmem((total, 1), jnp.float32),
-            vmem((total, 1), jnp.float32),
-            vmem((total, 1), jnp.float32),
+            vmem((total, 128), jnp.float32),
+            vmem((total, 128), jnp.float32),
+            vmem((total, 128), jnp.float32),
             vmem((NZ, 4, 128), jnp.float32),
             vmem((NZ, 4, 128), jnp.float32),
             vmem((2, 128), jnp.float32),
             vmem((NT, 2, 128), jnp.float32),
             dma,
-            dma((2, half)), dma((2, half)),
+            dma((2, half, rows // PIECE)), dma((2, half, rows // PIECE)),
             dma((2, half)), dma((2, half)),
             dma((3,)), dma((3,)),
             dma((3, 2)), dma((3, 2)),
@@ -358,8 +366,7 @@
         compiler_params=pltpu.CompilerParams(
             collective_id=0, has_side_effects=True, vmem_limit_bytes=60 * 1024 * 1024
         ),
-    )(hidden, norm_gain.reshape(1, width), head_weight, meta, lengths)
-    return out[0, :rows], out[1, :rows], out[2, :seqs], out[3, :seqs]
+    )(hidden, norm_gain, head_weight, token_order, targets, lengths)
 
 
 def solution(mesh):

time: 97.5 us -> 82.2 us (0.84)
  the two profiles are of different devices: /device:TPU:1 before, /device:TPU:2 now
where the time goes in v2:
time: 82.2 us; the launch traced here: 82 us
  Pallas kernels  76.8 us (93%)
  local copies, waits for them, and re-layouts  4.57 us (6%)
    pallas_call x1, Pallas kernels, per_device(): pl.pallas_call(kernel, out_shape=[jax.ShapeDtypeStruct((n,), jnp.float32)...  76.8 us
    unnamed x4, local copies, waits for them, and re-layouts  4.57 us

profile of v2, /device:TPU:2, one launch (start us, length us, event | category | flops | bytes accessed | tf_op | source)
XLA Modules:
  0.0 82.0 jit_solution(16565591551954616812)
XLA Ops:
  0.6 76.8 %shard_map.93 = (f32[48]{0:T(128)}, f32[48]{0:T(128)}, f32[8]{0:T(128)}, f32[8]{0:T(128)}) custom-call(bf16[48,1536]{1,0:T(8,128)(2,1)} %hid.1, bf16[1536]{0:T(1024)(128)(2,1)} %gain.1, bf16[1536,768]{1,0:T(8,128)(2,1)} %w_hbm.1, s32[48]{0:T(128)} %order_in.1, s32[48]{0:T(128)} %target_in.1, s32[8]{0:T(128)} %lengths.1), custom_call_target="tpu_custom_call" | custom-call | tf_op jit(solution)/shard_map/pallas_call | solution.py:334
  77.5 1.1 %copy.14 = f32[48]{0:T(128)} copy(f32[48]{0:T(128)} %get-tuple-element.8) | data formatting | bytes 384
  78.6 1.1 %copy.15 = f32[48]{0:T(128)} copy(f32[48]{0:T(128)} %get-tuple-element.9) | data formatting | bytes 384
  79.7 1.2 %copy.16 = f32[8]{0:T(128)} copy(f32[8]{0:T(128)} %get-tuple-element.10) | data formatting | bytes 64
  80.9 1.1 %copy.17 = f32[8]{0:T(128)} copy(f32[8]{0:T(128)} %get-tuple-element.11) | data formatting | bytes 64

commit v3 on v2

--- a/solution.py
+++ b/solution.py
@@ -15,13 +15,13 @@
 
 
 def kernel(
-    hid, gain, w_hbm, order_in, target_in, lengths, out_logprob, out_entropy, out_seq_logprob, out_seq_entropy,
-    xs, wb, lg, meta, thi, tlo, mx, sm, wt, st, stg, fing, fin,
+    hid_in, gain_in, w_hbm, order_in, target_in, lengths_in, out,
+    hid, gain, order_own, target_own, lengths, in_sem, xs, wb, lg, meta, thi, tlo, mx, sm, wt, st, stg, fing, fin,
     own_sem, tok_s, tok_r, met_s, met_r, my_s, my_r, wy_s, wy_r, wx_s, wx_r, wp_s, wp_r, b_s, b_r, c_s, c_r,
 ):
-    rows, width = hid.shape
+    rows, width = hid_in.shape
     depth, cols = w_hbm.shape
-    seqs = lengths.shape[0]
+    seqs = lengths_in.shape[0]
     dp, tt = lax.axis_index("dp"), lax.axis_index("tensor")
     core, x = lax.rem(dp, 2), lax.div(dp, 2)
     y, z = lax.rem(tt, NY), lax.div(tt, NY)
@@ -48,11 +48,21 @@
     for friend in friends:
         pl.semaphore_signal(barrier, inc=1, device_id=friend, device_id_type=MESH)
     own_copy = pltpu.make_async_copy(w_hbm, wb.at[3], own_sem)
+    inputs = [
+        pltpu.make_async_copy(source, target, in_sem.at[i])
+        for i, (source, target) in enumerate((
+            (hid_in, hid), (gain_in, gain), (order_in, order_own), (target_in, target_own), (lengths_in, lengths),
+        ))
+    ]
+    for copy in inputs:
+        copy.start()
     own_copy.start()
+    for copy in inputs:
+        copy.wait()
     meta[tt, 0:1, :] = jnp.full((1, 128), -1, jnp.int32)
     meta[tt, 1:2, :] = jnp.zeros((1, 128), jnp.int32)
-    meta[tt, 0:1, 0:rows] = order_in[...].reshape(1, rows)
-    meta[tt, 1:2, 0:rows] = target_in[...].reshape(1, rows)
+    meta[tt, 0:1, 0:rows] = order_own[...].reshape(1, rows)
+    meta[tt, 1:2, 0:rows] = target_own[...].reshape(1, rows)
     values = hid[...].astype(jnp.float32)
     scale = lax.rsqrt(jnp.mean(values * values, axis=-1, keepdims=True) + 1e-05)
     xs[0:rows, :] = (values * scale * gain[...].astype(jnp.float32).reshape(1, width)).astype(jnp.bfloat16)
@@ -71,8 +81,10 @@
             where = way, k - 1, piece
             return send(slot(source, piece), slot(target, piece), tok_s.at[where], tok_r.at[where], dev(dz=dz))
 
+        if k == NZ // 2:
+            return (one(piece % 2, 2 * k - 3 + piece % 2, 2 * k - 1, 1 - 2 * (piece % 2)),)
         right = one(0, max(2 * k - 3, 0), 2 * k - 1, 1)
-        return (right, one(1, 2 * k - 2, 2 * k, -1)) if k < NZ // 2 else (right,)
+        return right, one(1, 2 * k - 2, 2 * k, -1)
 
     def send_meta(k):
         there = meta.at[pl.ds(lax.rem(z - (k - 1) + NZ, NZ) * NY, NY)]
@@ -122,7 +134,7 @@
         here = pl.ds(first, count)
 
         def step(i, carry):
-            r = r_first + i
+            r = lax.rem(r_first + i, 4)
             logits = jnp.dot(xs[here, :], wb[r], preferred_element_type=jnp.float32)
             parts = [logits[:, c:c + 128] for c in range(0, cols, 128)]
             lg[r, here, :] = logits
@@ -153,20 +165,25 @@
         copy.wait_recv()
     metas[1] = send_meta(1)
 
-    def ring(k):
+    def ring_meta(k):
         for copy in metas[k]:
             if copy is not None:
                 copy.wait_recv()
         if k < NZ // 2:
             metas[k + 1] = send_meta(k + 1)
+
+    def ring_rows(k):
         for piece in range(pieces):
             for copy in tokens[k, piece]:
                 copy.wait_recv()
             if k < NZ // 2:
                 tokens[k + 1, piece] = send_tokens(k + 1, piece)
 
-    near, mid = 5 * rows, 11 * rows
-    total_rows = NZ * rows
+    def ring(k):
+        ring_meta(k)
+        ring_rows(k)
+
+    near, mid, far = 5 * rows, 9 * rows, 13 * rows
     ring(1)
     got_y(0, 0)
     got_y(1, 1)
@@ -179,23 +196,24 @@
     got_x(0, 0)
     got_x(1, 1)
     ring(4)
-    ring(5)
-    job(near, mid - near, 3, 1)
     got_y(2, 0)
     got_y(2, 1)
     got_x(0, 1)
     got_x(1, 0)
-    ring(6)
+    job(near, mid - near, 3, 1)
+    ring(5)
     got_partner(0)
     got_partner(1)
-    job(0, mid, 0, 2)
-    ring(7)
+    job(0, mid, 0, 1)
+    ring(6)
     got_x(2, 0)
     got_x(2, 1)
+    job(0, mid, 1, 1)
+    job(mid, far - mid, 3, 3)
+    ring(7)
     got_partner(2)
-    job(0, mid, 2, 1)
-    ring(8)
-    job(mid, total_rows - mid, 0, 4)
+    job(0, far, 2, 1)
+    ring_meta(8)
 
     lane = lax.broadcasted_iota(jnp.int32, (rows, 128), 1)
     eye = lane == lax.broadcasted_iota(jnp.int32, (rows, 128), 0)
@@ -219,37 +237,51 @@
             theirs, dz = 2 * k - 1, k
         stats.append(send(st.at[s], stg.at[theirs], b_s.at[s], b_r.at[theirs], dev(dz=dz)))
 
-    for s in range(NZ - 1, -1, -1):
-        k = (s + 1) // 2
-        zs = lax.rem(z + (-k if s % 2 else k) + NZ, NZ)
-        order = meta[zs * NY + y, 0:1, :]
-        order = jnp.sum(jnp.where(eye, order.astype(jnp.float32), 0.0), axis=1, keepdims=True).astype(jnp.int32)
-        inside = (order >= lane * rows) & (order < lane * rows + rows)
+    def finish_all(first, count):
+        slots, here = range(first, first + count), pl.ds(first * rows, count * rows)
+        orders = []
+        for s in slots:
+            k = (s + 1) // 2
+            zs = lax.rem(z + (-k if s % 2 else k) + NZ, NZ)
+            orders.append(jnp.where(eye, meta[zs * NY + y, 0:1, :].astype(jnp.float32), 0.0))
+        order = jnp.sum(jnp.concatenate(orders, axis=0), axis=1, keepdims=True).astype(jnp.int32)
+        lanes = lax.broadcasted_iota(jnp.int32, (count * rows, 128), 1)
+        ahead = order - lanes * rows
+        inside = (ahead >= 0) & (ahead < rows)
         picked = jnp.where(inside, 1.0, 0.0).astype(jnp.bfloat16)
         ids = 256.0 * jnp.dot(picked, high_ids, preferred_element_type=jnp.float32) + jnp.dot(
             picked, low_ids, preferred_element_type=jnp.float32
         )
-        start = jnp.sum(jnp.where(inside, (lane * rows).astype(jnp.float32), 0.0), axis=1, keepdims=True)
-        wanted = jnp.sum(
-            jnp.where(lane == order - start.astype(jnp.int32), ids, 0.0), axis=1, keepdims=True
-        ).astype(jnp.int32)
-        here = slice(s * rows, (s + 1) * rows)
-        found = jnp.zeros((rows, 128), jnp.float32)
-        for r in range(4):
-            near_wanted = wanted - (z * NY + lax.rem(y + OFFSETS[r], NY)) * cols
-            for c in range(0, cols, 128):
-                found += jnp.where(lane == near_wanted - c, lg[r, here, c:c + 128], 0.0)
-        target = jnp.sum(found, axis=-1, keepdims=True)
+        place_in = jnp.sum(jnp.where(inside, ahead.astype(jnp.float32), 0.0), axis=1, keepdims=True)
+        wanted = jnp.sum(jnp.where(lanes == place_in.astype(jnp.int32), ids, 0.0), axis=1, keepdims=True)
+        gap = wanted.astype(jnp.int32) - lanes
+        founds = []
+        for i, s in enumerate(slots):
+            own_gap = gap[i * rows:(i + 1) * rows, :]
+            found = jnp.zeros((rows, 128), jnp.float32)
+            for r in range(4):
+                base = (z * NY + lax.rem(y + OFFSETS[r], NY)) * cols
+                for c in range(0, cols, 128):
+                    found += jnp.where(own_gap == base + c, lg[r, s * rows:(s + 1) * rows, c:c + 128], 0.0)
+            founds.append(found)
+        target = jnp.sum(jnp.concatenate(founds, axis=0), axis=1, keepdims=True)
         lane_peak = mx[here, :]
-        peak = jnp.max(lane_peak, axis=-1, keepdims=True)
+        peak = jnp.max(lane_peak, axis=1, keepdims=True)
         fade = jnp.exp(lane_peak - peak)
-        place = stg if s == 0 else st
-        place[s, 0:1, :] = to_row(peak)
-        place[s, 1:2, :] = to_row(jnp.sum(sm[here, :] * fade, axis=-1, keepdims=True))
-        place[s, 2:3, :] = to_row(jnp.sum(wt[here, :] * fade, axis=-1, keepdims=True))
-        place[s, 3:4, :] = to_row(target)
-        if s + 1 < NZ:
-            send_stats(s + 1)
+        total = jnp.sum(sm[here, :] * fade, axis=1, keepdims=True)
+        weighted = jnp.sum(wt[here, :] * fade, axis=1, keepdims=True)
+        for i, s in enumerate(slots):
+            place = stg if s == 0 else st
+            for row, column in enumerate((peak, total, weighted, target)):
+                place[s, row:row + 1, :] = to_row(column[i * rows:(i + 1) * rows, :])
+        for s in reversed(slots):
+            if s:
+                send_stats(s)
+
+    finish_all(0, far // rows)
+    ring_rows(8)
+    job(far, NZ * rows - far, 0, 4)
+    finish_all(far // rows, NZ - far // rows)
 
     for copy in stats:
         copy.wait_recv()
@@ -315,12 +347,12 @@
 
     wide, narrow = jnp.zeros((rows, 128), jnp.float32), jnp.zeros((seqs, 128), jnp.float32)
     logprob, entropy, seq_logprob, seq_entropy = lax.fori_loop(0, NT, place_rows, (wide, wide, narrow, narrow))
-    out_logprob[...] = to_row(jnp.sum(logprob, axis=1, keepdims=True))[0, :rows]
-    out_entropy[...] = to_row(jnp.sum(entropy, axis=1, keepdims=True))[0, :rows]
+    out[0:1, :] = to_row(jnp.sum(logprob, axis=1, keepdims=True))
+    out[1:2, :] = to_row(jnp.sum(entropy, axis=1, keepdims=True))
     counts = (last - first).astype(jnp.float32)
-    for ref, value in ((out_seq_logprob, seq_logprob), (out_seq_entropy, seq_entropy)):
+    for i, value in ((2, seq_logprob), (3, seq_entropy)):
         mean = jnp.sum(value, axis=1, keepdims=True) / counts
-        ref[...] = jnp.sum(jnp.where(sub8 == lane8, mean, 0.0), axis=0, keepdims=True)[0, :seqs]
+        out[i:i + 1, :] = jnp.sum(jnp.where(sub8 == lane8, mean, 0.0), axis=0, keepdims=True)
 
 
 def per_device(hidden, norm_gain, head_weight, token_order, targets, lengths):
@@ -330,16 +362,18 @@
     total = NZ * rows
     vmem, dma = pltpu.VMEM, pltpu.SemaphoreType.DMA
     half = NZ // 2
-    in_vmem = pl.BlockSpec(memory_space=pltpu.VMEM)
-    return pl.pallas_call(
+    out = pl.pallas_call(
         kernel,
-        out_shape=[jax.ShapeDtypeStruct((n,), jnp.float32) for n in (rows, rows, seqs, seqs)],
-        in_specs=[
-            in_vmem, in_vmem, pl.BlockSpec(memory_space=pl.ANY), in_vmem, in_vmem,
-            pl.BlockSpec(memory_space=pltpu.SMEM),
-        ],
-        out_specs=[in_vmem] * 4,
+        out_shape=jax.ShapeDtypeStruct((4, 128), jnp.float32),
+        in_specs=[pl.BlockSpec(memory_space=pl.ANY)] * 6,
+        out_specs=pl.BlockSpec(memory_space=pltpu.VMEM),
         scratch_shapes=[
+            vmem(hidden.shape, hidden.dtype),
+            vmem(norm_gain.shape, norm_gain.dtype),
+            vmem((rows,), jnp.int32),
+            vmem((rows,), jnp.int32),
+            pltpu.SMEM((seqs,), jnp.int32),
+            dma((5,)),
             vmem((total, width), jnp.bfloat16),
             vmem((4, depth, cols), jnp.bfloat16),
             vmem((4, total, cols), jnp.float32),
@@ -367,6 +401,7 @@
             collective_id=0, has_side_effects=True, vmem_limit_bytes=60 * 1024 * 1024
         ),
     )(hidden, norm_gain, head_weight, token_order, targets, lengths)
+    return out[0, :rows], out[1, :rows], out[2, :seqs], out[3, :seqs]
 
 
 def solution(mesh):

time: 82.2 us -> 77.7 us (0.945)
  Pallas kernels: 76.8 us -> 74.4 us
  local copies, waits for them, and re-layouts: 4.57 us -> 2.49 us
    unnamed x4 -> x0, local copies, waits for them, and re-layouts: 4.57 us -> none
    squeeze x0 -> x2, local copies, waits for them, and re-layouts: none -> 2.49 us  [per_device(): return (out[0, :rows], out[1, :rows], out[2, :seqs], out[3, :seqs])]
    pallas_call x1, Pallas kernels: 76.8 us -> 74.4 us  [per_device(): pl.pallas_call(kernel, out_shape=jax.ShapeDtypeStruct((4, 128), jnp.float...]
where the time goes in v3:
time: 77.7 us; the launch traced here: 77.5 us
  Pallas kernels  74.4 us (96%)
  local copies, waits for them, and re-layouts  2.49 us (3%)
    pallas_call x1, Pallas kernels, per_device(): pl.pallas_call(kernel, out_shape=jax.ShapeDtypeStruct((4, 128), jnp.float...  74.4 us
    squeeze x2, local copies, waits for them, and re-layouts, per_device(): return (out[0, :rows], out[1, :rows], out[2, :seqs], out[3, :seqs])  2.49 us

profile of v3, /device:TPU:2, one launch (start us, length us, event | category | flops | bytes accessed | tf_op | source)
XLA Modules:
  0.0 77.5 jit_solution(16592543119312820381)
XLA Ops:
  0.6 74.4 %shard_map.93 = f32[4,128]{1,0:T(4,128)} custom-call(bf16[48,1536]{1,0:T(8,128)(2,1)} %hid_in.1, bf16[1536]{0:T(1024)(128)(2,1)} %gain_in.1, bf16[1536,768]{1,0:T(8,128)(2,1)} %w_hbm.1, s32[48]{0:T(128)} %order_in.1, s32[48]{0:T(128)} %target_in.1, s32[8]{0:T(128)} %lengths_in.1), custom_call_target="tpu_custom_call" | custom-call | tf_op jit(solution)/shard_map/pallas_call | solution.py:365
  75.0 1.2 %slice_bitcast_fusion = (f32[8]{0:T(128)}, f32[8]{0:T(128)}) fusion(f32[4,128]{1,0:T(4,128)} %shard_map.93), kind=kLoop, calls=%fused_computation | loop fusion | bytes 128 | tf_op jit(solution)/shard_map/squeeze | solution.py:404
  76.3 1.2 %slice_bitcast_fusion.2 = (f32[48]{0:T(128)}, f32[48]{0:T(128)}) fusion(f32[4,128]{1,0:T(4,128)} %shard_map.93), kind=kLoop, calls=%fused_computation.2 | loop fusion | bytes 768 | tf_op jit(solution)/shard_map/squeeze | solution.py:404

commit v4 on v3

--- a/solution.py
+++ b/solution.py
@@ -11,6 +11,7 @@
 NX, NY, NZ = 4, 4, 16
 NT = NZ * NY
 PIECE = 16
+SIDES = 1
 OFFSETS = (NY - 1, 1, 2, 0)
 
 
@@ -74,17 +75,21 @@
     pl.semaphore_wait(barrier, len(friends))
 
     def slot(s, piece):
-        return xs.at[pl.ds(s * rows + piece * PIECE, PIECE), :]
-
-    def send_tokens(k, piece):
-        def one(way, source, target, dz):
-            where = way, k - 1, piece
-            return send(slot(source, piece), slot(target, piece), tok_s.at[where], tok_r.at[where], dev(dz=dz))
-
-        if k == NZ // 2:
-            return (one(piece % 2, 2 * k - 3 + piece % 2, 2 * k - 1, 1 - 2 * (piece % 2)),)
-        right = one(0, max(2 * k - 3, 0), 2 * k - 1, 1)
-        return right, one(1, 2 * k - 2, 2 * k, -1)
+        band, side = piece // SIDES, piece % SIDES
+        return xs.at[pl.ds(s * rows + band * PIECE, PIECE), pl.ds(side * (width // SIDES), width // SIDES)]
+
+    def ways(k, piece):
+        return (0, 1) if k < NZ // 2 else (piece % 2,)
+
+    def send_tokens(k, piece, way):
+        if way not in ways(k, piece):
+            return
+        source = (2 * k - 2 if way else max(2 * k - 3, 0))
+        target = 2 * k if way and k < NZ // 2 else 2 * k - 1
+        where = way, k - 1, piece
+        tokens[where] = send(
+            slot(source, piece), slot(target, piece), tok_s.at[where], tok_r.at[where], dev(dz=-1 if way else 1)
+        )
 
     def send_meta(k):
         there = meta.at[pl.ds(lax.rem(z - (k - 1) + NZ, NZ) * NY, NY)]
@@ -151,8 +156,11 @@
 
         lax.fori_loop(0, r_count, step, 0)
 
-    pieces = rows // PIECE
-    tokens = {(1, piece): send_tokens(1, piece) for piece in range(pieces)}
+    pieces = rows // PIECE * SIDES
+    tokens = {}
+    for piece in range(pieces):
+        for way in (0, 1):
+            send_tokens(1, piece, way)
     metas = {}
     meta_y = [
         send(meta.at[tt], meta.at[tt], my_s.at[i], my_r.at[i], dev(dy=dy)) for i, dy in enumerate((1, -1, 2))
@@ -174,10 +182,10 @@
 
     def ring_rows(k):
         for piece in range(pieces):
-            for copy in tokens[k, piece]:
-                copy.wait_recv()
-            if k < NZ // 2:
-                tokens[k + 1, piece] = send_tokens(k + 1, piece)
+            for way in ways(k, piece):
+                tokens[way, k - 1, piece].wait_recv()
+                if k < NZ // 2:
+                    send_tokens(k + 1, piece, way)
 
     def ring(k):
         ring_meta(k)
@@ -308,11 +316,11 @@
             device_id=(dp, other), device_id_type=MESH,
         )
 
-    def start_final(i, carry):
-        final_copy(i).start()
+    def start_final(j, carry):
+        final_copy(1 + lax.rem(j + 24, NT - 1)).start()
         return carry
 
-    lax.fori_loop(1, NT, start_final, 0)
+    lax.fori_loop(0, NT - 1, start_final, 0)
     sub8 = lax.broadcasted_iota(jnp.int32, (seqs, 128), 0)
     lane8 = lax.broadcasted_iota(jnp.int32, (seqs, 128), 1)
     first = jnp.zeros((seqs, 128), jnp.int32)
@@ -346,7 +354,9 @@
         )
 
     wide, narrow = jnp.zeros((rows, 128), jnp.float32), jnp.zeros((seqs, 128), jnp.float32)
-    logprob, entropy, seq_logprob, seq_entropy = lax.fori_loop(0, NT, place_rows, (wide, wide, narrow, narrow))
+    logprob, entropy, seq_logprob, seq_entropy = lax.fori_loop(
+        0, NT, place_rows, (wide, wide, narrow, narrow), unroll=4
+    )
     out[0:1, :] = to_row(jnp.sum(logprob, axis=1, keepdims=True))
     out[1:2, :] = to_row(jnp.sum(entropy, axis=1, keepdims=True))
     counts = (last - first).astype(jnp.float32)
@@ -388,7 +398,7 @@
             vmem((2, 128), jnp.float32),
             vmem((NT, 2, 128), jnp.float32),
             dma,
-            dma((2, half, rows // PIECE)), dma((2, half, rows // PIECE)),
+            dma((2, half, rows // PIECE * SIDES)), dma((2, half, rows // PIECE * SIDES)),
             dma((2, half)), dma((2, half)),
             dma((3,)), dma((3,)),
             dma((3, 2)), dma((3, 2)),

time: 77.7 us -> 76.8 us (0.988)
  the two profiles are of different devices: /device:TPU:2 before, /device:TPU:32 now
where the time goes in v4:
time: 76.8 us; the launch traced here: 76.6 us
  Pallas kernels  73.5 us (96%)
  local copies, waits for them, and re-layouts  2.49 us (3%)
    pallas_call x1, Pallas kernels, per_device(): pl.pallas_call(kernel, out_shape=jax.ShapeDtypeStruct((4, 128), jnp.float...  73.5 us
    squeeze x2, local copies, waits for them, and re-layouts, per_device(): return (out[0, :rows], out[1, :rows], out[2, :seqs], out[3, :seqs])  2.49 us

profile of v4, /device:TPU:32, one launch (start us, length us, event | category | flops | bytes accessed | tf_op | source)
XLA Modules:
  0.0 76.6 jit_solution(5278071748723070787)
XLA Ops:
  0.6 73.5 %shard_map.93 = f32[4,128]{1,0:T(4,128)} custom-call(bf16[48,1536]{1,0:T(8,128)(2,1)} %hid_in.1, bf16[1536]{0:T(1024)(128)(2,1)} %gain_in.1, bf16[1536,768]{1,0:T(8,128)(2,1)} %w_hbm.1, s32[48]{0:T(128)} %order_in.1, s32[48]{0:T(128)} %target_in.1, s32[8]{0:T(128)} %lengths_in.1), custom_call_target="tpu_custom_call" | custom-call | tf_op jit(solution)/shard_map/pallas_call | solution.py:375
  74.1 1.2 %slice_bitcast_fusion = (f32[8]{0:T(128)}, f32[8]{0:T(128)}) fusion(f32[4,128]{1,0:T(4,128)} %shard_map.93), kind=kLoop, calls=%fused_computation | loop fusion | bytes 128 | tf_op jit(solution)/shard_map/squeeze | solution.py:414
  75.4 1.2 %slice_bitcast_fusion.2 = (f32[48]{0:T(128)}, f32[48]{0:T(128)}) fusion(f32[4,128]{1,0:T(4,128)} %shard_map.93), kind=kLoop, calls=%fused_computation.2 | loop fusion | bytes 768 | tf_op jit(solution)/shard_map/squeeze | solution.py:414
